TPU v7x, 512 devices: a whole 4x8x8 slice. The times are simulated.
512 devices in a mesh: dp: 8 (over y_hi, core), mp: 64 (over z, x, y_lo).
Axes of the slice: x: 4, y: 8 (y_hi: 4, y_lo: 2; y = y_hi * 2 + y_lo), z: 8, core: 2. Of those that a mesh axis runs over, the one named last changes fastest.
Arguments:
- queries: bfloat16 [65536, 768], P(('dp', 'mp')), may hold values from -30 to 30
- first_owner: int32 [65536, 1], P(('dp', 'mp')), may hold values from 0 to 63; in each aligned block of 128 rows (0 to 127, 128 to 255, ...) at most 4 rows name the same one
- first_row: int32 [65536], P(('dp', 'mp')), may hold values from 0 to 255
- tool_table: bfloat16 [16384, 768], P('mp'), may hold values from -6 to 6
- norm_gain: bfloat16 [768], replicated, may hold values from 0.25 to 1.75
- weight_in: bfloat16 [3072, 768], P('mp'), may hold values from -0.21875 to 0.21875
- bias_in: bfloat16 [3072], P('mp'), may hold values from -3 to 3
- weight_out: bfloat16 [3072, 768], P('mp'), may hold values from -0.109375 to 0.109375
- bias_out: bfloat16 [768], replicated, may hold values from -3 to 3
- tool_embeds: bfloat16 [512, 768], P('dp'), may hold values from -2 to 2
- positive: int32 [65536], P(('dp', 'mp')), may hold values from 0 to 511
Outputs:
- updated: bfloat16 [65536, 768], P(('dp', 'mp'))
- chain_loss: float32 [65536], P(('dp', 'mp'))
- query_grad: float32 [65536, 768], P(('dp', 'mp'))
- tool_grad: float32 [512, 768], P('dp')
Inputs may be any that keep to these rules, and one draw needn't show every extreme that they name: `first_owner`: among the 128 chains of one device at most 4 name the same owner, a bound that some block reaches of them.
All inputs are finite; a program needn't handle non-finite values.
Results may differ from a plain program's by a relative error of at most 0.0078.
Values may be sent and summed in bfloat16 or wider, within the bound.
A program may use at most 64 MiB of HBM per device.

v0:
```python
import jax
import jax.numpy as jnp
import numpy as np
from jax import lax
from jax.sharding import PartitionSpec as P


def from_behind(block, axis, distance):
    devices = range(lax.axis_size(axis))
    route = [((i - distance) % len(devices), i) for i in devices]
    return lax.ppermute(block, axis, route)


def layer_normed(combined, norm_gain):
    row_mean = jnp.mean(combined, axis=1, keepdims=True)
    centred = combined - row_mean
    spread = jnp.mean(centred * centred, axis=1, keepdims=True)
    return (centred * lax.rsqrt(spread + 1e-05) * norm_gain.astype(jnp.float32)[None, :]).astype(
        jnp.bfloat16
    )


def hidden_terms(pieces, normed):
    in_piece, bias_piece, out_piece = pieces
    preact = lax.dot_general(
        normed, in_piece, (((1,), (1,)), ((), ())), preferred_element_type=jnp.float32
    )
    preact = preact + bias_piece.astype(jnp.float32)[None, :]
    activated = jax.nn.gelu(preact, approximate=True).astype(jnp.bfloat16)
    return jnp.dot(activated, out_piece, preferred_element_type=jnp.float32)


def local(
    queries,
    first_owner,
    first_row,
    tool_table,
    norm_gain,
    weight_in,
    bias_in,
    weight_out,
    bias_out,
    tool_embeds,
    positive,
):
    chain_count, feature_count = queries.shape
    groups = lax.axis_size("mp")
    cycle_size = lax.axis_size("dp")
    cycle_index = lax.axis_index("dp")
    capacity = 2 * chain_count // groups
    owner_ids = first_owner[:, 0]
    owner_marks = (owner_ids[:, None] == jnp.arange(groups, dtype=jnp.int32)[None, :]).astype(
        jnp.int32
    )
    rank_in_owner = jnp.sum((jnp.cumsum(owner_marks, axis=0) - owner_marks) * owner_marks, axis=1)
    slot_index = owner_ids * capacity + rank_in_owner
    request = (
        jnp.zeros((groups * capacity,), jnp.int32)
        .at[slot_index]
        .set(first_row)
        .reshape(groups, capacity)
    )
    table_rows = jnp.take(
        tool_table, lax.all_to_all(request, "mp", split_axis=0, concat_axis=0, tiled=True), axis=0
    )
    fetched = lax.all_to_all(table_rows, "mp", split_axis=0, concat_axis=0, tiled=True)
    first_rows = fetched.reshape(groups * capacity, feature_count)[slot_index]
    combined = queries.astype(jnp.float32) + first_rows.astype(jnp.float32)
    normed = layer_normed(combined, norm_gain)
    branch_sum = hidden_terms(
        (
            lax.all_gather(weight_in, "mp", axis=0, tiled=True),
            lax.all_gather(bias_in, "mp", axis=0, tiled=True),
            lax.all_gather(weight_out, "mp", axis=0, tiled=True),
        ),
        normed,
    )
    updated = (combined + branch_sum + bias_out.astype(jnp.float32)[None, :]).astype(jnp.bfloat16)
    block_rows = tool_embeds.shape[0]
    forward_hops = cycle_size - 1
    block_list = [tool_embeds]
    offset_list = [0]
    visiting = tool_embeds
    for hop_number in range(forward_hops):
        visiting = from_behind(visiting, "dp", 1)
        block_list.append(visiting)
        offset_list.append(hop_number + 1)
    all_tools = jnp.concatenate(block_list, axis=0)
    block_owner = (cycle_index - jnp.asarray(offset_list, jnp.int32)) % cycle_size
    column_ids = (
        block_owner[:, None] * block_rows + jnp.arange(block_rows, dtype=jnp.int32)[None, :]
    ).reshape(-1)
    scores = lax.dot_general(
        updated, all_tools, (((1,), (1,)), ((), ())), preferred_element_type=jnp.float32
    )
    row_max = jnp.max(scores, axis=1, keepdims=True)
    log_total = row_max + jnp.log(jnp.sum(jnp.exp(scores - row_max), axis=1, keepdims=True))
    is_positive = (column_ids[None, :] == positive[:, None]).astype(jnp.float32)
    chain_loss = log_total[:, 0] - jnp.sum(scores * is_positive, axis=1)
    weights_grad = (jnp.exp(scores - log_total) - is_positive).astype(jnp.bfloat16)
    query_grad = jnp.dot(weights_grad, all_tools, preferred_element_type=jnp.float32)
    position_of = np.zeros((cycle_size,), np.int32)
    for list_index, offset_value in enumerate(offset_list):
        position_of[offset_value] = list_index

    def block_term(offset_value):
        list_index = int(position_of[offset_value])
        columns = weights_grad[:, list_index * block_rows : (list_index + 1) * block_rows]
        return lax.dot_general(
            columns, updated, (((0,), (0,)), ((), ())), preferred_element_type=jnp.float32
        )

    partial_grad = jnp.zeros((block_rows, feature_count), jnp.float32)
    for hop_number in range(cycle_size - 1):
        partial_grad = partial_grad + block_term(hop_number + 1)
        partial_grad = from_behind(partial_grad.astype(jnp.bfloat16), "dp", 1).astype(
            partial_grad.dtype
        )
    partial_grad = partial_grad + block_term(0)
    grad_scale = (block_rows * cycle_size / (chain_count * groups * cycle_size)) ** 0.5
    tool_grad = lax.psum(partial_grad, "mp") * grad_scale
    return (updated, chain_loss, query_grad, tool_grad)


def solution(mesh):
    in_specs = (
        P(("dp", "mp"), None),
        P(("dp", "mp"), None),
        P(("dp", "mp")),
        P("mp", None),
        P(),
        P("mp", None),
        P("mp"),
        P("mp", None),
        P(),
        P("dp", None),
        P(("dp", "mp")),
    )
    out_specs = (P(("dp", "mp"), None), P(("dp", "mp")), P(("dp", "mp"), None), P("dp", None))
    return jax.shard_map(local, mesh=mesh, in_specs=in_specs, out_specs=out_specs, check_vma=False)
```

profile of v0, /device:TPU:16, one launch (start us, length us, event | category | flops | bytes accessed | tf_op | source)
XLA Modules:
  0.0 1266.2 jit_solution(13888815105655201328)
XLA Ops:
  7.2 0.7 all-gather.3.cloned.1.call-update
  8.0 0.7 all-gather.5.cloned.1.call-update
  8.7 0.7 fusion.20
  9.6 0.8 select_reduce_fusion
  10.4 0.7 fusion.40
  11.1 1.1 scatter_custom_fusion
  12.2 0.7 all_to_all.13
  12.9 14.8 %all-to-all-start = ((s32[64,1,4]{2,1,0:T(1,128)}), s32[64,1,4]{2,1,0:T(1,128)S(1)}, u32[]{:S(2)}, u32[]{:S(2)}) async-start(s32[64,1,4]{2,1,0:T(1,128)} %bitcast.3), calls=%async_computation | async-start | bytes 65536 | tf_op jit(solution)/shard_map/all_to_all | solution.py:64
  27.7 1.9 collective-permute-start
  29.7 1.3 dynamic-slice
  31.6 0.9 dynamic-update-slice
  32.5 0.9 constant_dynamic-update-slice_fusion.7
  33.4 163.7 %all-reduce = bf16[3072]{0:T(1024)(128)(2,1)S(1)} all-reduce(bf16[3072]{0:T(1024)(128)(2,1)S(1)} %dynamic-update-slice), channel_id=1, replica_groups=mesh['dp'=8,'mp'=64] {'mp'}, use_global_device_ids=true, to_apply=%add | all-reduce | flops 3072 | bytes 12288
  197.2 0.7 convert_element_type.78
  197.9 0.7 convert_element_type.82
  198.8 1.2 gather_fusion
  200.1 1.0 broadcast_select_fusion
  201.1 5.3 all-to-all-start.1
  206.5 1.9 collective-permute-start.1
  208.5 6.4 collective-permute-done.1
  214.9 2.1 collective-permute-start.2
  217.0 7.5 collective-permute-done.2
  224.4 1.9 collective-permute-start.3
  226.4 6.5 collective-permute-done.3
  232.9 1.9 collective-permute-start.4
  234.8 5.5 collective-permute-done.4
  240.3 4.1 collective-permute-start.5
  244.4 4.4 collective-permute-done.5
  248.8 3.8 collective-permute-start.6
  252.7 5.0 collective-permute-done.6
  257.8 0.9 gather_fusion.1
  258.8 0.2 multiply_reduce_fusion
  259.1 72.0 %all-gather.3.cloned.1.call-done = bf16[3072,768]{1,0:T(8,128)(2,1)} async-done(((bf16[48,768]{1,0:T(8,128)(2,1)}), bf16[3072,768]{1,0:T(8,128)(2,1)}) %all-gather.3.cloned.1.call-update) | async-done | bytes 4718608 | tf_op jit(solution)/shard_map/all_gather | solution.py:72
  331.1 314.4 %all-gather.5.cloned.1.call-done = bf16[3072,768]{1,0:T(8,128)(2,1)} async-done(((bf16[48,768]{1,0:T(8,128)(2,1)}), bf16[3072,768]{1,0:T(8,128)(2,1)}) %all-gather.5.cloned.1.call-update) | async-done | bytes 4718608 | tf_op jit(solution)/shard_map/all_gather | solution.py:74
  645.5 6.2 fusion.9
  651.8 0.5 fusion.48
  652.2 0.2 fusion.11
  652.5 0.5 fusion.47
  653.1 0.3 convolution_convert_fusion
  653.4 1.9 collective-permute-start.7
  655.3 5.7 collective-permute-done.7
  661.0 0.2 add_convert_fusion.5
  661.2 1.9 collective-permute-start.8
  663.1 0.3 fusion.31
  663.4 5.7 collective-permute-done.8
  669.1 1.9 collective-permute-start.9
  671.0 0.2 fusion.29
  671.2 5.8 collective-permute-done.9
  677.0 1.9 collective-permute-start.10
  678.9 0.3 fusion.27
  679.2 5.7 collective-permute-done.10
  684.9 2.1 collective-permute-start.11
  687.0 0.2 fusion.25
  687.2 4.6 collective-permute-done.11
  691.8 3.3 collective-permute-start.12
  695.0 0.3 fusion.23
  695.3 3.3 collective-permute-done.12
  698.6 4.5 collective-permute-start.13
  703.1 0.2 fusion.21
  703.3 2.2 collective-permute-done.13
  705.5 0.7 convert_add_fusion.3
  706.2 1.0 fusion.49
  707.2 550.8 %all-reduce.3.cloned.1.call-done = f32[64,768]{1,0:T(8,128)} async-done(((f32[64,768]{1,0:T(8,128)}), f32[64,768]{1,0:T(8,128)}) %all-reduce.3.cloned.1.call-update) | async-done | bytes 196624 | tf_op jit(solution)/shard_map/psum | solution.py:121
  1258.0 1.6 broadcast_multiply_fusion
  (44 shorter events, 1.3 us)
Async XLA Ops:
  7.2 191.6 %copy-start = (bf16[256,768]{1,0:T(8,128)(2,1)S(1)}, bf16[256,768]{1,0:T(8,128)(2,1)}, u32[]{:S(2)}) copy-start(bf16[256,768]{1,0:T(8,128)(2,1)} %param.15) | copy-start | bytes 1179652
  7.2 323.9 %all-gather.3.cloned.1.call-start = ((), (), s32[]{:S(2)}) async-start(), calls=%async_computation.2 | async-start | bytes 4792320 | tf_op jit(solution)/shard_map/all_gather | solution.py:72
  7.9 637.6 %all-gather.5.cloned.1.call-start = ((), (), s32[]{:S(2)}) async-start(), calls=%async_computation.3 | async-start | bytes 4792320 | tf_op jit(solution)/shard_map/all_gather | solution.py:74
  12.9 185.7 %all-to-all-start = ((s32[64,1,4]{2,1,0:T(1,128)}), s32[64,1,4]{2,1,0:T(1,128)S(1)}, u32[]{:S(2)}, u32[]{:S(2)}) async-start(s32[64,1,4]{2,1,0:T(1,128)} %bitcast.3), calls=%async_computation | async-start | bytes 65536 | tf_op jit(solution)/shard_map/all_to_all | solution.py:64
  27.7 178.8 %collective-permute-start = (bf16[64,768]{1,0:T(8,128)(2,1)}, bf16[64,768]{1,0:T(8,128)(2,1)S(1)}, u32[]{:S(2)}, u32[]{:S(2)}) collective-permute-start(bf16[64,768]{1,0:T(8,128)(2,1)} %param.21), channel_id=1, source_target_pairs={{448,0},{0,64},{64,128},{128,192},{192,256},{256,320},{320,384},{3... | collective-permute-start | bytes 294920 | tf_op jit(solution)/shard_map/ppermute | solution.py:11
  201.1 56.6 %all-to-all-start.1 = ((bf16[64,4,768]{2,1,0:T(4,128)(2,1)}), bf16[64,4,768]{2,1,0:T(4,128)(2,1)S(1)}, u32[]{:S(2)}, u32[]{:S(2)}) async-start(bf16[64,4,768]{2,1,0:T(4,128)(2,1)} %broadcast_select_fusion), calls=%async_computation.1 | async-start | bytes 786432 | tf_op jit(solution)/shard_map/all_to_all | solution.py:66
  206.5 1051.5 %all-reduce.3.cloned.1.call-start = ((), (), s32[]{:S(2)}) async-start(), calls=%async_computation.4 | async-start | bytes 393216 | tf_op jit(solution)/shard_map/psum | solution.py:121
  206.5 8.4 collective-permute-start.1
  214.9 9.5 collective-permute-start.2
  224.4 8.4 collective-permute-start.3
  232.9 7.4 collective-permute-start.4
  234.8 23.9 %copy-start.2 = (bf16[128,768]{1,0:T(8,128)(2,1)S(1)}, bf16[128,768]{1,0:T(8,128)(2,1)}, u32[]{:S(2)}) copy-start(bf16[128,768]{1,0:T(8,128)(2,1)} %param.12) | copy-start | bytes 589828
  240.3 8.5 collective-permute-start.5
  248.8 8.9 collective-permute-start.6
  259.0 393.2 %copy-start.3 = (s32[128]{0:T(128)S(1)}, s32[128]{0:T(128)}, u32[]{:S(2)}) copy-start(s32[128]{0:T(128)} %param.22) | copy-start | bytes 1540
  651.7 51.4 %copy-start.1 = (bf16[128,768]{1,0:T(8,128)(2,1)}, bf16[128,768]{1,0:T(8,128)(2,1)S(1)}, u32[]{:S(2)}) copy-start(bf16[128,768]{1,0:T(8,128)(2,1)S(1)} %fusion.9) | copy-start | bytes 589828
  653.4 7.6 collective-permute-start.7
  661.2 7.9 collective-permute-start.8
  669.1 7.9 collective-permute-start.9
  677.0 7.9 collective-permute-start.10
  684.9 6.8 collective-permute-start.11
  691.8 6.8 collective-permute-start.12
  698.6 6.8 collective-permute-start.13
Sparse Core Ops, SparseCore 0:
  10.1 320.9 all-gather.2
  333.2 312.3 all-gather.4
  706.3 551.6 all-reduce.2
where the time goes:
time: 1270 us
  waiting for transfers between devices  1010 us (80%)
  blocking collectives  164 us (13%)
  starting transfers between devices  55.3 us (4%)
  between operations  14.9 us (1%)
    psum x1, waiting for transfers between devices, local(): tool_grad = lax.psum(partial_grad, 'mp') * grad_scale  551 us
    all_gather x1, waiting for transfers between devices, local(): lax.all_gather(weight_out, 'mp', axis=0, tiled=True)  314 us
    unnamed x1, blocking collectives  164 us
    all_gather x1, waiting for transfers between devices, local(): lax.all_gather(weight_in, 'mp', axis=0, tiled=True)  72 us
    ppermute x14, waiting for transfers between devices, from_behind(): return lax.ppermute(block, axis, route)  68.2 us
    ppermute x14, starting transfers between devices, from_behind(): return lax.ppermute(block, axis, route)  35.1 us
  transfers between devices with their start and end apart: 19, of which 16 were waited for; matrix products, arithmetic and copies ran while one was open for 1% of the time, Pallas kernels for 0%

commit v1 on v0

--- a/solution.py
+++ b/solution.py
@@ -1,8 +1,16 @@
+import functools
 import jax
 import jax.numpy as jnp
 import numpy as np
 from jax import lax
 from jax.sharding import PartitionSpec as P
+
+
+def _set_zones(unit, comm_axis):
+    return jnp.sum(jax.lax.all_gather(unit, comm_axis), axis=0)
+
+
+spread_tracks = functools.partial(_set_zones, comm_axis="mp")
 
 
 def from_behind(block, axis, distance):
@@ -118,7 +126,7 @@
         )
     partial_grad = partial_grad + block_term(0)
     grad_scale = (block_rows * cycle_size / (chain_count * groups * cycle_size)) ** 0.5
-    tool_grad = lax.psum(partial_grad, "mp") * grad_scale
+    tool_grad = spread_tracks(partial_grad) * grad_scale
     return (updated, chain_loss, query_grad, tool_grad)
 
 

time: 1270 us -> 1070 us (0.84)
  waiting for transfers between devices: 1010 us -> 804 us
    psum x1 -> x0, waiting for transfers between devices: 551 us -> none  [local(): tool_grad = lax.psum(partial_grad, 'mp') * grad_scale]
    all_gather x0 -> x1, waiting for transfers between devices: none -> 350 us  [_set_zones(): return jnp.sum(jax.lax.all_gather(unit, comm_axis), axis=0)]
where the time goes in v1:
time: 1070 us
  waiting for transfers between devices  804 us (75%)
  blocking collectives  164 us (15%)
  starting transfers between devices  57.2 us (5%)
  between operations  14.8 us (1%)
  other arithmetic  12.8 us (1%)
    all_gather x1, waiting for transfers between devices, _set_zones(): return jnp.sum(jax.lax.all_gather(unit, comm_axis), axis=0)  350 us
    all_gather x1, waiting for transfers between devices, local(): lax.all_gather(weight_out, 'mp', axis=0, tiled=True)  313 us
    unnamed x1, blocking collectives  164 us
    all_gather x1, waiting for transfers between devices, local(): lax.all_gather(weight_in, 'mp', axis=0, tiled=True)  73.3 us
    ppermute x14, waiting for transfers between devices, from_behind(): return lax.ppermute(block, axis, route)  66.4 us
    ppermute x14, starting transfers between devices, from_behind(): return lax.ppermute(block, axis, route)  36.8 us
  transfers between devices with their start and end apart: 19, of which 16 were waited for; matrix products, arithmetic and copies ran while one was open for 1% of the time, Pallas kernels for 0%

profile of v1, /device:TPU:16, one launch (start us, length us, event | category | flops | bytes accessed | tf_op | source)
XLA Modules:
  0.0 1069.3 jit_solution(13411108609109826895)
XLA Ops:
  7.2 0.7 all-gather.5.cloned.1.call-update
  8.0 0.7 all-gather.7.cloned.1.call-update
  8.7 0.7 fusion.20
  9.6 0.8 select_reduce_fusion
  10.4 0.7 fusion.40
  11.1 1.1 scatter_custom_fusion
  12.2 0.7 all_to_all.13
  12.9 14.8 %all-to-all-start = ((s32[64,1,4]{2,1,0:T(1,128)}), s32[64,1,4]{2,1,0:T(1,128)S(1)}, u32[]{:S(2)}, u32[]{:S(2)}) async-start(s32[64,1,4]{2,1,0:T(1,128)} %bitcast.3), calls=%async_computation | async-start | bytes 65536 | tf_op jit(solution)/shard_map/all_to_all | solution.py:72
  27.7 1.9 collective-permute-start
  29.7 1.3 dynamic-slice
  31.6 0.9 dynamic-update-slice
  32.5 0.9 constant_dynamic-update-slice_fusion.7
  33.4 163.7 %all-reduce = bf16[3072]{0:T(1024)(128)(2,1)S(1)} all-reduce(bf16[3072]{0:T(1024)(128)(2,1)S(1)} %dynamic-update-slice), channel_id=1, replica_groups=mesh['dp'=8,'mp'=64] {'mp'}, use_global_device_ids=true, to_apply=%add | all-reduce | flops 3072 | bytes 12288
  197.2 0.7 convert_element_type.78
  197.9 0.7 convert_element_type.82
  198.7 1.2 gather_fusion
  200.1 1.0 broadcast_select_fusion
  201.1 5.5 all-to-all-start.1
  206.6 1.9 collective-permute-start.1
  208.6 6.5 collective-permute-done.1
  215.1 1.9 collective-permute-start.2
  217.0 7.6 collective-permute-done.2
  224.7 1.9 collective-permute-start.3
  226.6 6.0 collective-permute-done.3
  232.6 2.1 collective-permute-start.4
  234.7 5.4 collective-permute-done.4
  240.1 5.1 collective-permute-start.5
  245.2 3.8 collective-permute-done.5
  249.0 4.5 collective-permute-start.6
  253.5 4.2 collective-permute-done.6
  257.8 0.9 gather_fusion.1
  258.8 0.2 multiply_reduce_fusion
  259.0 73.3 %all-gather.5.cloned.1.call-done = bf16[3072,768]{1,0:T(8,128)(2,1)} async-done(((bf16[48,768]{1,0:T(8,128)(2,1)}), bf16[3072,768]{1,0:T(8,128)(2,1)}) %all-gather.5.cloned.1.call-update) | async-done | bytes 4718608 | tf_op jit(solution)/shard_map/all_gather | solution.py:80
  332.3 312.6 %all-gather.7.cloned.1.call-done = bf16[3072,768]{1,0:T(8,128)(2,1)} async-done(((bf16[48,768]{1,0:T(8,128)(2,1)}), bf16[3072,768]{1,0:T(8,128)(2,1)}) %all-gather.7.cloned.1.call-update) | async-done | bytes 4718608 | tf_op jit(solution)/shard_map/all_gather | solution.py:82
  644.9 6.2 fusion.9
  651.1 0.5 fusion.48
  651.6 0.2 fusion.11
  651.8 0.5 fusion.47
  652.5 0.3 convolution_convert_fusion
  652.8 1.9 collective-permute-start.7
  654.7 5.7 collective-permute-done.7
  660.4 0.2 add_convert_fusion.5
  660.6 1.9 collective-permute-start.8
  662.5 0.3 fusion.31
  662.8 5.7 collective-permute-done.8
  668.5 1.9 collective-permute-start.9
  670.4 0.2 fusion.29
  670.6 5.8 collective-permute-done.9
  676.4 1.9 collective-permute-start.10
  678.3 0.3 fusion.27
  678.6 5.7 collective-permute-done.10
  684.3 2.1 collective-permute-start.11
  686.6 4.6 collective-permute-done.11
  691.2 3.3 collective-permute-start.12
  694.4 0.3 fusion.23
  694.7 3.3 collective-permute-done.12
  698.0 4.5 collective-permute-start.13
  702.5 0.2 fusion.21
  702.7 2.2 collective-permute-done.13
  704.9 0.7 convert_add_fusion.3
  705.6 1.0 fusion.49
  706.6 350.3 %all-gather.9.cloned.1.call-done = f32[4096,768]{1,0:T(8,128)} async-done(((f32[64,768]{1,0:T(8,128)}), f32[4096,768]{1,0:T(8,128)}) %all-gather.9.cloned.1.call-update) | async-done | bytes 12582928 | tf_op jit(solution)/shard_map/all_gather | solution.py:10
  1056.9 5.2 reduce_sum.62
  1062.1 0.7 broadcast_multiply_fusion
  (45 shorter events, 1.4 us)
Async XLA Ops:
  7.2 191.6 %copy-start = (bf16[256,768]{1,0:T(8,128)(2,1)S(1)}, bf16[256,768]{1,0:T(8,128)(2,1)}, u32[]{:S(2)}) copy-start(bf16[256,768]{1,0:T(8,128)(2,1)} %param.15) | copy-start | bytes 1179652
  7.2 325.1 %all-gather.5.cloned.1.call-start = ((), (), s32[]{:S(2)}) async-start(), calls=%async_computation.2 | async-start | bytes 4792320 | tf_op jit(solution)/shard_map/all_gather | solution.py:80
  7.9 637.0 %all-gather.7.cloned.1.call-start = ((), (), s32[]{:S(2)}) async-start(), calls=%async_computation.3 | async-start | bytes 4792320 | tf_op jit(solution)/shard_map/all_gather | solution.py:82
  12.9 185.7 %all-to-all-start = ((s32[64,1,4]{2,1,0:T(1,128)}), s32[64,1,4]{2,1,0:T(1,128)S(1)}, u32[]{:S(2)}, u32[]{:S(2)}) async-start(s32[64,1,4]{2,1,0:T(1,128)} %bitcast.3), calls=%async_computation | async-start | bytes 65536 | tf_op jit(solution)/shard_map/all_to_all | solution.py:72
  27.7 178.9 %collective-permute-start = (bf16[64,768]{1,0:T(8,128)(2,1)}, bf16[64,768]{1,0:T(8,128)(2,1)S(1)}, u32[]{:S(2)}, u32[]{:S(2)}) collective-permute-start(bf16[64,768]{1,0:T(8,128)(2,1)} %param.21), channel_id=1, source_target_pairs={{448,0},{0,64},{64,128},{128,192},{192,256},{256,320},{320,384},{3... | collective-permute-start | bytes 294920 | tf_op jit(solution)/shard_map/ppermute | solution.py:19
  201.1 56.6 %all-to-all-start.1 = ((bf16[64,4,768]{2,1,0:T(4,128)(2,1)}), bf16[64,4,768]{2,1,0:T(4,128)(2,1)S(1)}, u32[]{:S(2)}, u32[]{:S(2)}) async-start(bf16[64,4,768]{2,1,0:T(4,128)(2,1)} %broadcast_select_fusion), calls=%async_computation.1 | async-start | bytes 786432 | tf_op jit(solution)/shard_map/all_to_all | solution.py:74
  206.6 850.3 %all-gather.9.cloned.1.call-start = ((), (), s32[]{:S(2)}) async-start(), calls=%async_computation.4 | async-start | bytes 12779520 | tf_op jit(solution)/shard_map/all_gather | solution.py:10
  206.6 8.5 collective-permute-start.1
  215.1 9.6 collective-permute-start.2
  224.7 7.9 collective-permute-start.3
  232.6 7.5 collective-permute-start.4
  234.6 24.0 %copy-start.2 = (bf16[128,768]{1,0:T(8,128)(2,1)S(1)}, bf16[128,768]{1,0:T(8,128)(2,1)}, u32[]{:S(2)}) copy-start(bf16[128,768]{1,0:T(8,128)(2,1)} %param.12) | copy-start | bytes 589828
  240.1 8.9 collective-permute-start.5
  249.0 8.7 collective-permute-start.6
  259.0 392.6 %copy-start.3 = (s32[128]{0:T(128)S(1)}, s32[128]{0:T(128)}, u32[]{:S(2)}) copy-start(s32[128]{0:T(128)} %param.22) | copy-start | bytes 1540
  651.1 51.4 %copy-start.1 = (bf16[128,768]{1,0:T(8,128)(2,1)}, bf16[128,768]{1,0:T(8,128)(2,1)S(1)}, u32[]{:S(2)}) copy-start(bf16[128,768]{1,0:T(8,128)(2,1)S(1)} %fusion.9) | copy-start | bytes 589828
  652.8 7.6 collective-permute-start.7
  660.6 7.9 collective-permute-start.8
  668.5 7.9 collective-permute-start.9
  676.4 7.9 collective-permute-start.10
  684.3 6.8 collective-permute-start.11
  691.2 6.8 collective-permute-start.12
  698.0 6.8 collective-permute-start.13
Sparse Core Ops, SparseCore 0:
  10.1 322.1 all-gather.4
  334.4 310.4 all-gather.6
  705.7 351.1 all-gather.8
